TPU v7x, 256 devices: a whole 4x4x8 slice. The times are simulated.
256 devices in a mesh: blk: 8 (over x_hi, y), rep: 32 (over z, x_lo, core).
Axes of the slice: x: 4 (x_hi: 2, x_lo: 2; x = x_hi * 2 + x_lo), y: 4, z: 8, core: 2. Of those that a mesh axis runs over, the one named last changes fastest.
Arguments:
- query_hidden: bfloat16 [32, 32, 32, 768], P('rep', 'blk'), may hold values from -18 to 18
- passage_hidden: bfloat16 [32, 32, 512, 768], P('rep', 'blk'), may hold values from -6 to 6
- lengths: int32 [32, 32], P('rep', 'blk'), may hold values from 64 to 512
- projection: bfloat16 [768, 128], replicated, may hold values from -0.21875 to 0.21875
Outputs:
- query_grad: float32 [32, 32, 32, 128], P('rep', 'blk')
- passage_grad: float32 [32, 32, 512, 128], P('rep', 'blk')
- grad_weight: float32 [768, 128], replicated
- loss: float32 [], replicated
All inputs are finite; a program needn't handle non-finite values.
Results may differ from a plain program's by a relative error of at most 0.0097.
Values may be sent and summed in bfloat16 or wider, within the bound.
No kernel may reach another device: no remote copies, remote signals or barrier semaphores. Data moves between devices by JAX's collectives and lax.ppermute only.
A program may use at most 128 MiB of HBM per device.

v0:
```python
import jax
import jax.numpy as jnp
from jax import lax
from jax.sharding import PartitionSpec as P

temper = 0.5


def soft_scores(scores, lens):
    slots = scores.shape[-1]
    valid = lax.broadcasted_iota(jnp.int32, (lens.shape[0], slots), 1) < lens[:, None]
    scaled = jnp.where(valid[None], scores / temper, -jnp.inf)
    top = jnp.max(scaled, -1, keepdims=True)
    logz = top + jnp.log(jnp.sum(jnp.exp(scaled - top), -1, keepdims=True))
    pooled = temper * (logz[..., 0] - jnp.log(lens.astype(jnp.float32))[None])
    return (pooled, scaled, logz)


def cross_entropy(score, first, total):
    top = jnp.max(score, 1, keepdims=True)
    lse = top + jnp.log(jnp.sum(jnp.exp(score - top), 1, keepdims=True))
    target = lax.broadcasted_iota(jnp.int32, score.shape, 1) == first + lax.broadcasted_iota(
        jnp.int32, score.shape, 0
    )
    loss_part = jnp.sum(lse[:, 0] - jnp.sum(jnp.where(target, score, 0.0), 1))
    dscore = (jnp.exp(score - lse) - target.astype(jnp.float32)) / total
    return (loss_part, dscore)


def weighted(dscore, scaled, logz, qlen):
    spread = jnp.repeat(dscore, qlen, axis=0)
    grad_a = (spread[:, :, None] * jnp.exp(scaled - logz)).astype(jnp.bfloat16)
    return grad_a.reshape(grad_a.shape[0], -1)


def shards(query_hidden, passage_hidden, lengths, projection):
    hidden = projection.shape[0]
    nquery = query_hidden.shape[1]
    qlen = query_hidden.shape[2]
    npass = passage_hidden.shape[1]
    plen = passage_hidden.shape[2]
    groups = lax.axis_size("blk")
    total = groups * lax.axis_size("rep") * nquery
    first = lax.axis_index("blk") * nquery
    qflat = query_hidden[0].reshape(-1, hidden)
    pflat = passage_hidden[0].reshape(-1, hidden)
    qtok = jnp.dot(qflat, projection, preferred_element_type=jnp.float32).astype(jnp.bfloat16)
    ptok = jnp.dot(pflat, projection, preferred_element_type=jnp.float32).astype(jnp.bfloat16)
    every_tok = lax.all_gather(ptok, "blk", axis=0, tiled=True)
    every_len = lax.all_gather(lengths[0], "blk", axis=0, tiled=True)
    scores = jnp.dot(qtok, every_tok.T, preferred_element_type=jnp.float32).reshape(
        nquery * qlen, groups * npass, plen
    )
    pooled, scaled, logz = soft_scores(scores, every_len)
    score = jnp.sum(pooled.reshape(nquery, qlen, groups * npass), 1)
    loss_part, dscore = cross_entropy(score, first, total)
    grad_a = weighted(dscore, scaled, logz, qlen)
    qgrad = jnp.dot(grad_a, every_tok, preferred_element_type=jnp.float32)
    pgrad = lax.psum_scatter(
        jnp.dot(grad_a.T, qtok, preferred_element_type=jnp.float32),
        "blk",
        scatter_dimension=0,
        tiled=True,
    )
    wgrad = jnp.dot(qflat.T, qgrad.astype(jnp.bfloat16), preferred_element_type=jnp.float32)
    wgrad = wgrad + jnp.dot(pflat.T, pgrad.astype(jnp.bfloat16), preferred_element_type=jnp.float32)
    wgrad, loss_sum = lax.psum((wgrad, loss_part), ("blk", "rep"))
    query_grad = qgrad.reshape(1, nquery, qlen, -1)
    passage_grad = pgrad.reshape(1, npass, plen, -1)
    return (query_grad, passage_grad, wgrad, loss_sum / total)


def solution(mesh):
    return jax.shard_map(
        shards,
        mesh=mesh,
        in_specs=(P("rep", "blk", None, None), P("rep", "blk", None, None), P("rep", "blk"), P()),
        out_specs=(P("rep", "blk", None, None), P("rep", "blk", None, None), P(), P()),
        check_vma=False,
    )
```

profile of v0, /device:TPU:1, one launch (start us, length us, event | category | flops | bytes accessed | tf_op | source)
XLA Modules:
  0.0 521.1 jit_solution(17235841440828739490)
XLA Ops:
  7.2 1.8 copy-done
  9.1 2.7 convolution_convert_fusion
  11.9 1.3 dynamic-slice
  13.8 0.8 bitcast_dynamic-update-slice_fusion
  14.6 11.6 %all-reduce = s32[32]{0:T(128)S(1)} all-reduce(s32[32]{0:T(128)S(1)} %bitcast_dynamic-update-slice_fusion), channel_id=2, replica_groups=mesh['blk'=8,'rep'=32] {'blk'}, use_global_device_ids=true, to_apply=%add | all-reduce | flops 32 | bytes 256 | tf_op jit(solution)/shard_map/all_gather | solution.py:50
  26.4 1.2 convolution_convert_fusion.1
  27.6 64.1 %all-gather.3.cloned.1.call-done = bf16[16384,128]{1,0:T(8,128)(2,1)} async-done(((bf16[2048,128]{1,0:T(8,128)(2,1)}), bf16[16384,128]{1,0:T(8,128)(2,1)}) %all-gather.3.cloned.1.call-update) | async-done | bytes 4194320 | tf_op jit(solution)/shard_map/all_gather | solution.py:49
  91.8 3.4 convolution_multiply_fusion
  95.2 6.5 %copy.9 = f32[16,8,32,512]{3,2,1,0:T(8,128)S(1)} copy(f32[16,8,32,512]{3,1,2,0:T(8,128)S(1)} %bitcast.36) | data formatting | bytes 16777216
  102.5 2.3 exponential_reduce_fusion
  105.8 0.7 mul.27
  106.5 9.7 %copy.10 = f32[16,8,32,512]{3,1,2,0:T(8,128)} copy(f32[16,8,32,512]{3,2,1,0:T(8,128)S(1)} %bitcast.43) | data formatting | bytes 16777216
  116.2 0.9 sub.59
  117.2 9.8 %copy.12 = f32[16,8,32,512]{3,1,2,0:T(8,128)} copy(f32[16,8,32,512]{3,2,1,0:T(8,128)S(1)} %bitcast.44) | data formatting | bytes 16777216
  126.9 7.0 %multiply_convert_fusion = bf16[128,16384]{1,0:T(8,128)(2,1)S(1)} fusion(f32[128,16384]{1,0:T(8,128)} %bitcast.41, f32[128,16384]{1,0:T(8,128)} %bitcast.42, f32[128,16384]{1,0:T(8,128)S(1)} %bitcast.38, pred[16384]{0:T(1024)(128)(4,1)S(1)} %lt.23), kind=kLoop, calls=%fused_computation.1 | loop fusion | flops 8388608 | bytes 29376512 | tf_op jit(solution)/shard_map/convert_element_type | solution.py:32
  134.0 2.0 copy-done.2
  136.0 4.5 fusion.5
  140.6 4.7 fusion.4
  145.3 112.7 %reduce-scatter.2.cloned.1.call-done = f32[2048,128]{1,0:T(8,128)} async-done(((f32[16384,128]{1,0:T(8,128)}), f32[2048,128]{1,0:T(8,128)}) %reduce-scatter.2.cloned.1.call-update) | async-done | bytes 1048592 | tf_op jit(solution)/shard_map/reduce_scatter | solution.py:59
  258.1 1.8 fusion.1
  259.9 1.0 fusion
  260.9 74.6 %psum.15 = f32[]{:T(128)} all-reduce(f32[]{:T(128)} %get-tuple-element.10), channel_id=1, replica_groups=mesh['blk'=8,'rep'=32] {'blk','rep'}, use_global_device_ids=true, to_apply=%region_9.10 | all-reduce | flops 1 | bytes 8 | tf_op jit(solution)/shard_map/psum | solution.py:67
  336.2 175.4 %all-reduce.3.cloned.1.call-done = f32[768,128]{0,1:T(8,128)} async-done(((f32[768,128]{0,1:T(8,128)}), f32[768,128]{0,1:T(8,128)}) %all-reduce.3.cloned.1.call-update) | async-done | bytes 393232 | tf_op jit(solution)/shard_map/psum | solution.py:67
  511.5 1.9 copy.8
  (34 shorter events, 2.2 us)
Async XLA Ops:
  7.2 1.9 copy-start
  7.2 84.6 %all-gather.3.cloned.1.call-start = ((), (), s32[]{:S(2)}) async-start(), calls=%async_computation.1 | async-start | bytes 4718592 | tf_op jit(solution)/shard_map/all_gather | solution.py:49
  11.8 246.3 %reduce-scatter.2.cloned.1.call-start = ((), (), s32[]{:S(2)}) async-start(), calls=%async_computation.2 | async-start | bytes 9437184 | tf_op jit(solution)/shard_map/reduce_scatter | solution.py:59
  95.2 6.5 %copy-start.1 = (f32[128,16384]{1,0:T(8,128)}, f32[128,16384]{1,0:T(8,128)S(1)}, u32[]{:S(2)}) copy-start(f32[128,16384]{1,0:T(8,128)S(1)} %convolution_multiply_fusion) | copy-start | bytes 25165828
  116.2 10.7 %slice-start = ((s8[8388608]{0:T(1024)(128)(4,1)}), s8[4194304]{0:T(1024)(128)(4,1)S(1)}, s32[]{:S(2)}) async-start(s8[8388608]{0:T(1024)(128)(4,1)} %bitcast.37), calls=%async_computation.4 | async-start | bytes 8388608
  117.2 9.8 %slice-start.1 = ((s8[8388608]{0:T(1024)(128)(4,1)}), s8[4194304]{0:T(1024)(128)(4,1)S(1)}, s32[]{:S(2)}) async-start(s8[8388608]{0:T(1024)(128)(4,1)} %bitcast.37), calls=%async_computation.5 | async-start | bytes 8388608
  134.0 2.0 copy-start.2
  140.5 119.4 %copy-start.3 = (bf16[1,4,32,768]{3,2,1,0:T(8,128)(2,1)S(1)}, bf16[1,4,32,768]{3,2,1,0:T(8,128)(2,1)}, u32[]{:S(2)}) copy-start(bf16[1,4,32,768]{3,2,1,0:T(8,128)(2,1)} %param.4) | copy-start | bytes 589828
  140.5 371.0 %all-reduce.3.cloned.1.call-start = ((), (), s32[]{:S(2)}) async-start(), calls=%async_computation.3 | async-start | bytes 786432 | tf_op jit(solution)/shard_map/psum | solution.py:67
  145.3 368.1 %copy-start.4 = (f32[128,128]{1,0:T(8,128)}, f32[128,128]{1,0:T(8,128)S(1)}, u32[]{:S(2)}) copy-start(f32[128,128]{1,0:T(8,128)S(1)} %fusion.4) | copy-start | bytes 196612
Sparse Core Ops, SparseCore 0:
  11.9 79.8 all-gather.2
  140.6 117.3 reduce-scatter.1
  265.1 246.4 all-reduce.2
where the time goes:
time: 522 us; the launch traced here: 521 us
  waiting for transfers between devices  352 us (67%)
  blocking collectives  86.2 us (17%)
  local copies, waits for them, and re-layouts  35.5 us (7%)
  matrix products  19.4 us (4%)
  between operations  16.4 us (3%)
  other arithmetic  11.2 us (2%)
    psum x1, waiting for transfers between devices, shards(): wgrad, loss_sum = lax.psum((wgrad, loss_part), ('blk', 'rep'))  175 us
    reduce_scatter x1, waiting for transfers between devices, shards(): lax.psum_scatter(jnp.dot(grad_a.T, qtok, preferred_element_type=jnp.float...  113 us
    psum x1, blocking collectives, shards(): wgrad, loss_sum = lax.psum((wgrad, loss_part), ('blk', 'rep'))  74.6 us
    all_gather x1, waiting for transfers between devices, shards(): every_tok = lax.all_gather(ptok, 'blk', axis=0, tiled=True)  64.1 us
    unnamed x23, local copies, waits for them, and re-layouts  33.8 us
    all_gather x1, blocking collectives, shards(): every_len = lax.all_gather(lengths[0], 'blk', axis=0, tiled=True)  11.6 us
  transfers between devices with their start and end apart: 3, of which 3 were waited for; matrix products, arithmetic and copies ran while one was open for 2% of the time, Pallas kernels for 0%

commit v1 on v0

--- a/solution.py
+++ b/solution.py
@@ -1,9 +1,27 @@
+import functools
 import jax
 import jax.numpy as jnp
 from jax import lax
 from jax.sharding import PartitionSpec as P
+from jax.lax import all_to_all, psum
 
 temper = 0.5
+
+
+def cut_runs(mine_x, peer_axis, dim_i):
+    z1 = jnp.concatenate(
+        all_to_all(
+            jnp.stack(psum(1, axis_name=peer_axis) * [mine_x]),
+            axis_name=peer_axis,
+            split_axis=0,
+            concat_axis=0,
+        ),
+        dim_i,
+    )
+    return z1
+
+
+finish_yards = functools.partial(cut_runs, peer_axis="blk", dim_i=0)
 
 
 def soft_scores(scores, lens):
@@ -46,7 +64,7 @@
     pflat = passage_hidden[0].reshape(-1, hidden)
     qtok = jnp.dot(qflat, projection, preferred_element_type=jnp.float32).astype(jnp.bfloat16)
     ptok = jnp.dot(pflat, projection, preferred_element_type=jnp.float32).astype(jnp.bfloat16)
-    every_tok = lax.all_gather(ptok, "blk", axis=0, tiled=True)
+    every_tok = finish_yards(ptok)
     every_len = lax.all_gather(lengths[0], "blk", axis=0, tiled=True)
     scores = jnp.dot(qtok, every_tok.T, preferred_element_type=jnp.float32).reshape(
         nquery * qlen, groups * npass, plen

time: 522 us -> 489 us (0.937)
  waiting for transfers between devices: 352 us -> 290 us
  blocking collectives: 86.2 us -> 128 us
  local copies, waits for them, and re-layouts: 35.5 us -> 14.2 us
  starting transfers between devices: 0.12 us -> 7.7 us
    all_gather x1 -> x0, waiting for transfers between devices: 64.1 us -> none  [shards(): every_tok = lax.all_gather(ptok, 'blk', axis=0, tiled=True)]
    all_gather x1, blocking collectives: 11.6 us -> 53.2 us  [shards(): every_len = lax.all_gather(lengths[0], 'blk', axis=0, tiled=True)]
    unnamed x23 -> x26, local copies, waits for them, and re-layouts: 33.8 us -> 5.03 us
    all_to_all x0 -> x1, starting transfers between devices: none -> 7.62 us  [cut_runs(): all_to_all(jnp.stack(psum(1, axis_name=peer_axis) * [mine_x]), axis_name=...]
    convert_element_type x0 -> x1, local copies, waits for them, and re-layouts: none -> 6.39 us  [weighted(): grad_a = (spread[:, :, None] * jnp.exp(scaled - logz)).astype(jnp.bfloat16)]
  transfers between devices with their start and end apart: 3 -> 3, of which waited for: 3 -> 2; matrix products, arithmetic and copies ran while one was open for 2% -> 2% of each run, Pallas kernels for 0% -> 0%
where the time goes in v1:
time: 489 us; the launch traced here: 488 us
  waiting for transfers between devices  290 us (59%)
  blocking collectives  128 us (26%)
  matrix products  20.5 us (4%)
  between operations  16.6 us (3%)
  local copies, waits for them, and re-layouts  14.2 us (3%)
  other arithmetic  11.2 us (2%)
  starting transfers between devices  7.7 us (2%)
    psum x1, waiting for transfers between devices, shards(): wgrad, loss_sum = lax.psum((wgrad, loss_part), ('blk', 'rep'))  175 us
    reduce_scatter x1, waiting for transfers between devices, shards(): lax.psum_scatter(jnp.dot(grad_a.T, qtok, preferred_element_type=jnp.float...  115 us
    psum x1, blocking collectives, shards(): wgrad, loss_sum = lax.psum((wgrad, loss_part), ('blk', 'rep'))  74.6 us
    all_gather x1, blocking collectives, shards(): every_len = lax.all_gather(lengths[0], 'blk', axis=0, tiled=True)  53.2 us
  transfers between devices with their start and end apart: 3, of which 2 were waited for; matrix products, arithmetic and copies ran while one was open for 2% of the time, Pallas kernels for 0%

profile of v1, /device:TPU:1, one launch (start us, length us, event | category | flops | bytes accessed | tf_op | source)
XLA Modules:
  0.0 488.0 jit_solution(17336181360967730487)
XLA Ops:
  7.2 1.9 copy-done
  9.1 1.9 convolution_convert_fusion
  11.0 2.5 stack.2
  13.4 7.6 %all-to-all-start = ((bf16[8,2048,128]{2,1,0:T(8,128)(2,1)}), bf16[8,2048,128]{2,1,0:T(8,128)(2,1)}, u32[]{:S(2)}, u32[]{:S(2)}) async-start(bf16[8,2048,128]{2,1,0:T(8,128)(2,1)} %stack.2), calls=%async_computation | async-start | bytes 8388608 | tf_op jit(solution)/shard_map/all_to_all | solution.py:13
  21.1 0.6 dynamic-slice
  22.5 53.2 %all-reduce = s32[32]{0:T(128)S(1)} all-reduce(s32[32]{0:T(128)S(1)} %bitcast_dynamic-update-slice_fusion), channel_id=2, replica_groups=mesh['blk'=8,'rep'=32] {'blk'}, use_global_device_ids=true, to_apply=%add | all-reduce | flops 32 | bytes 256 | tf_op jit(solution)/shard_map/all_gather | solution.py:68
  75.7 0.5 iota_add_fusion
  76.2 0.5 convert_log_fusion
  76.7 0.7 iota_compare_fusion
  77.5 0.8 convolution_convert_fusion.1
  78.3 3.5 fusion
  81.9 2.7 exponential_reduce_fusion
  84.6 0.5 copy-done.1
  85.5 0.6 subtract_reduce_fusion
  86.3 5.9 %multiply_convert_fusion = bf16[128,32,512]{2,0,1:T(8,128)(2,1)} fusion(f32[128,32,512]{2,0,1:T(8,128)} %copy-done.1, f32[128,32]{0,1:T(8,128)S(1)} %log_add_fusion, f32[128,32]{0,1:T(8,128)S(1)} %mul.23, pred[32,512]{1,0:T(8,128)(4,1)S(1)} %iota_compare_fusion), kind=kLoop, calls=%fused_computation | loop fusion | flops 10485760 | bytes 12632064 | tf_op jit(solution)/shard_map/convert_element_type | solution.py:50
  92.2 6.4 %copy.9 = bf16[128,32,512]{0,2,1:T(8,128)(2,1)} copy(bf16[128,32,512]{2,0,1:T(8,128)(2,1)} %multiply_convert_fusion) | data formatting | bytes 8388608 | tf_op jit(solution)/shard_map/convert_element_type | solution.py:50
  98.6 6.6 %fusion.8 = f32[16384,128]{1,0:T(8,128)} fusion(bf16[128,16384]{0,1:T(8,128)(2,1)} %bitcast.34, bf16[128,128]{1,0:T(8,128)(2,1)S(1)} %copy-done.4), kind=kOutput, calls=%fused_computation.26 | convolution fusion | flops 536870912 | bytes 12615680 | tf_op jit(solution)/shard_map/dot_general | solution.py:78
  105.3 4.8 fusion.7
  110.1 114.6 %reduce-scatter.2.cloned.1.call-done = f32[2048,128]{1,0:T(8,128)} async-done(((f32[16384,128]{1,0:T(8,128)}), f32[2048,128]{1,0:T(8,128)}) %reduce-scatter.2.cloned.1.call-update) | async-done | bytes 1048592 | tf_op jit(solution)/shard_map/reduce_scatter | solution.py:77
  224.6 1.8 fusion.2
  226.5 1.0 fusion.1
  227.5 74.6 %psum.15 = f32[]{:T(128)} all-reduce(f32[]{:T(128)} %get-tuple-element.14), channel_id=1, replica_groups=mesh['blk'=8,'rep'=32] {'blk','rep'}, use_global_device_ids=true, to_apply=%region_9.10 | all-reduce | flops 1 | bytes 8 | tf_op jit(solution)/shard_map/psum | solution.py:85
  302.7 175.3 %all-reduce.3.cloned.1.call-done = f32[768,128]{0,1:T(8,128)} async-done(((f32[768,128]{0,1:T(8,128)}), f32[768,128]{0,1:T(8,128)}) %all-reduce.3.cloned.1.call-update) | async-done | bytes 393232 | tf_op jit(solution)/shard_map/psum | solution.py:85
  478.1 1.9 copy.10
  (35 shorter events, 0.8 us)
Async XLA Ops:
  7.2 1.9 copy-start
  13.4 7.7 %copy-start.10 = (u32[256]{0:T(256)S(1)}, u32[256]{0:T(256)}, u32[]{:S(2)}) copy-start(u32[256]{0:T(256)} %constant.27) | copy-start | bytes 3076
  13.4 8.9 %copy-start.9 = (s32[1,4]{1,0:T(1,128)S(1)}, s32[1,4]{1,0:T(1,128)}, u32[]{:S(2)}) copy-start(s32[1,4]{1,0:T(1,128)} %param.6) | copy-start | bytes 52
  13.4 64.0 %copy-start.2 = (bf16[768,128]{1,0:T(8,128)(2,1)S(1)}, bf16[768,128]{1,0:T(8,128)(2,1)}, u32[]{:S(2)}) copy-start(bf16[768,128]{1,0:T(8,128)(2,1)} %param.7) | copy-start | bytes 589828
  13.4 64.1 %copy-start.3 = (bf16[1,4,32,768]{3,2,1,0:T(8,128)(2,1)S(1)}, bf16[1,4,32,768]{3,2,1,0:T(8,128)(2,1)}, u32[]{:S(2)}) copy-start(bf16[1,4,32,768]{3,2,1,0:T(8,128)(2,1)} %param.4) | copy-start | bytes 589828
  13.4 64.9 %all-to-all-start = ((bf16[8,2048,128]{2,1,0:T(8,128)(2,1)}), bf16[8,2048,128]{2,1,0:T(8,128)(2,1)}, u32[]{:S(2)}, u32[]{:S(2)}) async-start(bf16[8,2048,128]{2,1,0:T(8,128)(2,1)} %stack.2), calls=%async_computation | async-start | bytes 8388608 | tf_op jit(solution)/shard_map/all_to_all | solution.py:13
  21.1 203.6 %reduce-scatter.2.cloned.1.call-start = ((), (), s32[]{:S(2)}) async-start(), calls=%async_computation.2 | async-start | bytes 9437184 | tf_op jit(solution)/shard_map/reduce_scatter | solution.py:77
  75.7 0.5 copy-start.8
  81.9 3.2 copy-start.1
  81.9 3.3 copy-start.7
  81.9 3.5 copy-start.6
  92.2 6.4 %copy-start.4 = (bf16[128,128]{1,0:T(8,128)(2,1)S(1)}, bf16[128,128]{1,0:T(8,128)(2,1)}, u32[]{:S(2)}) copy-start(bf16[128,128]{1,0:T(8,128)(2,1)} %convolution_convert_fusion.1) | copy-start | bytes 98308
  105.2 372.8 %all-reduce.3.cloned.1.call-start = ((), (), s32[]{:S(2)}) async-start(), calls=%async_computation.3 | async-start | bytes 786432 | tf_op jit(solution)/shard_map/psum | solution.py:85
  110.0 369.9 %copy-start.5 = (f32[128,128]{1,0:T(8,128)}, f32[128,128]{1,0:T(8,128)S(1)}, u32[]{:S(2)}) copy-start(f32[128,128]{1,0:T(8,128)S(1)} %fusion.7) | copy-start | bytes 196612
Sparse Core Ops, SparseCore 0:
  105.4 119.2 reduce-scatter.1
  231.6 246.3 all-reduce.2
